TPU v7x, 512 devices: a whole 4x8x8 slice. The times are simulated.
512 devices in a mesh: snap: 32 (over z, x), vert: 16 (over y, core).
Axes of the slice: x: 4, y: 8, z: 8, core: 2. Of those that a mesh axis runs over, the one named last changes fastest.
Arguments:
- features: bfloat16 [32, 4096, 512], P('snap', 'vert'), may hold values from -6 to 6
- tile_values: bfloat16 [32, 32, 12, 128, 128], P('snap', 'vert'), may hold values from -0.21875 to 0.21875
- tile_column: int32 [32, 32, 12], P('snap', 'vert'), may hold values from 0 to 31
- tile_count: int32 [32, 32], P('snap', 'vert'), may hold values from 1 to 12, 192 in all within a row
- message_one: bfloat16 [512, 512], replicated, may hold values from -0.25 to 0.25
- root_one: bfloat16 [512, 512], replicated, may hold values from -0.25 to 0.25
- time_taps: float32 [16, 512], replicated, may hold values from -1.5 to 1.5
- message_two: bfloat16 [512, 512], replicated, may hold values from -0.25 to 0.25
- root_two: bfloat16 [512, 512], replicated, may hold values from -0.25 to 0.25
Outputs:
- embedding: bfloat16 [32, 4096, 512], P('snap', 'vert')
Inputs may be any that keep to these rules, and one draw needn't show every extreme that they name: `tile_count`: over one snapshot the counts sum to 192, and some row block has 12 live slots; slots at or past the count are ignored. `tile_column`: blocks may repeat within a row block's list.
All inputs are finite; a program needn't handle non-finite values.
Results may differ from a plain program's by a relative error of at most 0.0064.
Values may be sent and summed in bfloat16 or wider, within the bound.
No kernel may reach another device: no remote copies, remote signals or barrier semaphores. Data moves between devices by JAX's collectives and lax.ppermute only.
A program may use at most 64 MiB of HBM per device.

v0:
```python
import jax
import jax.numpy as jnp
from jax import lax
from jax.sharding import PartitionSpec as P

TILE = 128
TAPS = 16


def block_table(columns, counts, total_blocks):
    live = lax.broadcasted_iota(jnp.int32, columns.shape, 2) < counts[:, :, None]
    target = lax.broadcasted_iota(jnp.int32, columns.shape + (total_blocks,), 3)
    hits = (columns[:, :, :, None] == target) & live[:, :, :, None]
    return jnp.where(hits, 1.0, 0.0).astype(jnp.bfloat16)


def aggregate(messages, spread):
    snaps, rows, width = messages.shape
    tiles_all, table_all = spread
    split = lax.all_to_all(messages, "vert", split_axis=2, concat_axis=1, tiled=True)
    narrow = split.shape[2]
    verts = split.shape[1]
    blocks = split.reshape(snaps, verts // TILE, TILE, narrow)
    picked = jnp.einsum(
        "srkp,sptf->srktf", table_all, blocks, preferred_element_type=jnp.float32
    ).astype(jnp.bfloat16)
    summed = jnp.einsum("srkij,srkjf->srif", tiles_all, picked, preferred_element_type=jnp.float32)
    summed = summed.reshape(snaps, verts, narrow)
    return lax.all_to_all(summed, "vert", split_axis=1, concat_axis=2, tiled=True)


def graph_layer(inputs, w_message, w_root, spread):
    messages = jnp.einsum(
        "svf,fg->svg", inputs, w_message, preferred_element_type=jnp.float32
    ).astype(jnp.bfloat16)
    summed = aggregate(messages, spread)
    total = summed + jnp.einsum("svf,fg->svg", inputs, w_root, preferred_element_type=jnp.float32)
    return jnp.maximum(total, 0.0).astype(jnp.bfloat16)


def shards(
    features,
    tile_values,
    tile_column,
    tile_count,
    message_one,
    root_one,
    time_taps,
    message_two,
    root_two,
):
    table = block_table(tile_column, tile_count, tile_column.shape[1] * lax.axis_size("vert"))
    spread = None
    spread = (
        lax.all_gather(tile_values, "vert", axis=1, tiled=True),
        lax.all_gather(table, "vert", axis=1, tiled=True),
    )
    hidden = graph_layer(features, message_one, root_one, spread)
    by_vertex = lax.all_to_all(hidden, "snap", split_axis=1, concat_axis=0, tiled=True)
    steps_all, vrows, width = by_vertex.shape
    wide = by_vertex.astype(jnp.float32)
    padded = jnp.concatenate([jnp.zeros((TAPS - 1, vrows, width), jnp.float32), wide], 0)
    mixed = jnp.zeros((steps_all, vrows, width), jnp.float32)
    for offset in range(TAPS):
        mixed = (
            mixed
            + time_taps[offset][None, None, :]
            * padded[TAPS - 1 - offset : TAPS - 1 - offset + steps_all]
        )
    mixed = mixed.astype(jnp.bfloat16)
    returned = lax.all_to_all(mixed, "snap", split_axis=0, concat_axis=1, tiled=True)
    return graph_layer(returned, message_two, root_two, spread)


def solution(mesh):
    return jax.shard_map(
        shards,
        mesh=mesh,
        in_specs=(
            P("snap", "vert", None),
            P("snap", "vert", None, None, None),
            P("snap", "vert", None),
            P("snap", "vert"),
            P(),
            P(),
            P(),
            P(),
            P(),
        ),
        out_specs=P("snap", "vert", None),
        check_vma=False,
    )
```

profile of v0, /device:TPU:1, one launch (start us, length us, event | category | flops | bytes accessed | tf_op | source)
XLA Modules:
  0.0 287.5 jit_solution(12193270720602912220)
XLA Ops:
  6.5 0.0 copy-start
  6.5 0.0 all-gather.2.cloned.1.call-start
  6.5 0.7 all-gather.2.cloned.1.call-update
  7.3 0.3 copy-done
  7.6 1.2 fusion.20
  8.8 0.4 copy.21
  9.3 0.5 broadcast.55
  9.8 2.2 reduce
  12.0 0.8 reshape.151
  12.8 10.2 %all-to-all-start = ((bf16[16,2,4096]{2,1,0:T(2,128)(2,1)}), bf16[16,2,4096]{2,1,0:T(2,128)(2,1)S(1)}, u32[]{:S(2)}, u32[]{:S(2)}) async-start(bf16[16,2,4096]{2,1,0:T(2,128)(2,1)} %reshape.151), calls=%async_computation | async-start | bytes 524288 | tf_op jit(solution)/shard_map/all_to_all | solution.py:20
  22.9 0.1 iota_compare_fusion.1
  23.0 0.0 copy-done.4
  23.0 0.1 select_convert_fusion
  23.1 21.5 %all_gather.6 = bf16[1,32,12,32]{3,2,0,1:T(8,128)(2,1)S(1)} all-gather(bf16[1,2,12,32]{3,2,0,1:T(8,128)(2,1)S(1)} %select_convert_fusion), channel_id=1, replica_groups=mesh['snap'=32,'vert'=16] {'vert'}, dimensions={1}, use_global_device_ids=true | all-gather | bytes 26112 | tf_op jit(solution)/shard_map/all_gather | solution.py:56
  44.6 0.0 all-to-all-done
  44.6 0.3 reshape.152
  44.9 0.2 copy.22
  45.1 0.1 reshape.145
  45.2 2.6 convolution_convert_fusion.1
  47.8 46.8 %all-gather.2.cloned.1.call-done = bf16[1,32,12,128,128]{4,3,2,0,1:T(8,128)(2,1)} async-done(((bf16[1,2,12,128,128]{4,3,2,0,1:T(8,128)(2,1)}), bf16[1,32,12,128,128]{4,3,2,0,1:T(8,128)(2,1)}) %all-gather.2.cloned.1.call-update) | async-done | bytes 12582928 | tf_op jit(solution)/shard_map/all_gather | solution.py:55
  94.6 9.8 %fusion.6 = f32[32,128,32]{1,2,0:T(8,128)S(1)} fusion(bf16[1,32,12,128,128]{4,3,2,0,1:T(8,128)(2,1)} %all-gather.2.cloned.1.call-done, bf16[32,12,128,32]{2,0,3,1:T(8,128)(2,1)} %convolution_convert_fusion.1), kind=kOutput, calls=%fused_computation.23 | convolution fusion | flops 402653184 | bytes 16252928 | tf_op jit(solution)/shard_map/srkij,srkjf->srif/dot_general | solution.py:27
  104.4 0.6 copy.42
  105.0 0.6 broadcast.56
  105.6 19.4 %reduce.1 = f32[4096,32]{1,0:T(8,128)} reduce(f32[4096,1,32]{2,1,0:T(1,128)S(1)} %bitcast.110, f32[]{:T(128)} %broadcast.56), dimensions={1}, to_apply=%bitcast.90.reduce_sub_computation | reduce | bytes 1048580
  125.0 2.5 reshape.153
  127.4 21.6 %all_to_all.84 = f32[16,1,8192]{2,1,0:T(1,128)S(1)} all-to-all(f32[16,1,8192]{2,1,0:T(1,128)S(1)} %reshape.153), channel_id=1, replica_groups=mesh['snap'=32,'vert'=16] {'vert'}, dimensions={0} | all-to-all | bytes 1048576 | tf_op jit(solution)/shard_map/all_to_all | solution.py:29
  149.0 1.9 reduce.2
  150.9 0.0 copy-start.1
  150.9 3.5 %reshape.154 = f32[4096,1,32]{2,1,0:T(1,128)S(1)} reshape(f32[16,8192]{1,0:T(8,128)S(1)} %reduce.2) | data formatting | bytes 1048576
  154.4 0.7 copy.43
  155.1 0.0 copy-start.3
  155.1 0.3 copy.28
  155.5 0.2 copy.29
  155.7 1.3 fusion.23
  157.0 0.4 copy.70
  157.4 0.0 copy-start.2
  157.4 2.3 reduce.3
  159.7 0.8 reshape.155
  160.5 11.3 %all-to-all-start.2 = ((bf16[32,2,2048]{2,1,0:T(2,128)(2,1)}), bf16[32,2,2048]{2,1,0:T(2,128)(2,1)S(1)}, u32[]{:S(2)}, u32[]{:S(2)}) async-start(bf16[32,2,2048]{2,1,0:T(2,128)(2,1)} %reshape.155), calls=%async_computation.2 | async-start | bytes 524288 | tf_op jit(solution)/shard_map/all_to_all | solution.py:59
  171.9 12.7 %all-to-all-done.2 = bf16[32,2,2048]{2,1,0:T(2,128)(2,1)S(1)} async-done(((bf16[32,2,2048]{2,1,0:T(2,128)(2,1)}), bf16[32,2,2048]{2,1,0:T(2,128)(2,1)S(1)}, u32[]{:S(2)}, u32[]{:S(2)}) %all-to-all-start.2) | async-done | bytes 262176 | tf_op jit(solution)/shard_map/all_to_all | solution.py:59
  184.6 0.3 reshape.156
  184.8 0.5 bitcast_convert_fusion
  185.4 0.5 fusion.54
  185.9 15.1 %all_to_all.85 = bf16[32,8,512]{2,1,0:T(8,128)(2,1)S(1)} all-to-all(bf16[32,8,512]{2,1,0:T(8,128)(2,1)S(1)} %fusion.54), channel_id=1, replica_groups=mesh['snap'=32,'vert'=16] {'snap'}, dimensions={0} | all-to-all | bytes 524288 | tf_op jit(solution)/shard_map/all_to_all | solution.py:71
  201.0 0.3 fusion.21
  201.3 0.4 copy.31
  201.8 2.2 reduce.4
  204.0 0.1 reshape.157
  204.0 16.6 %all_to_all.86 = bf16[16,2,4096]{2,1,0:T(2,128)(2,1)S(1)} all-to-all(bf16[16,2,4096]{2,1,0:T(2,128)(2,1)S(1)} %reshape.157), channel_id=1, replica_groups=mesh['snap'=32,'vert'=16] {'vert'}, dimensions={0} | all-to-all | bytes 524288 | tf_op jit(solution)/shard_map/all_to_all | solution.py:20
  220.6 0.3 reshape.158
  221.0 0.2 copy.32
  221.1 0.1 reshape.147
  221.2 0.9 convolution_convert_fusion
  222.2 7.1 %fusion.11 = f32[32,128,32]{1,2,0:T(8,128)S(1)} fusion(bf16[1,32,12,128,128]{4,3,2,0,1:T(8,128)(2,1)} %all-gather.2.cloned.1.call-done, bf16[32,12,128,32]{2,0,3,1:T(8,128)(2,1)S(1)} %convolution_convert_fusion), kind=kOutput, calls=%fused_computation.24 | convolution fusion | flops 402653184 | bytes 16252928 | tf_op jit(solution)/shard_map/srkij,srkjf->srif/dot_general | solution.py:27
  229.2 0.6 copy.44
  229.9 19.4 %reduce.5 = f32[4096,32]{1,0:T(8,128)} reduce(f32[4096,1,32]{2,1,0:T(1,128)S(1)} %bitcast.111, f32[]{:T(128)} %broadcast.56), dimensions={1}, to_apply=%bitcast.96.reduce_sub_computation | reduce | bytes 1048580
  249.2 2.5 reshape.159
  251.7 20.1 %all_to_all.87 = f32[16,1,8192]{2,1,0:T(1,128)S(1)} all-to-all(f32[16,1,8192]{2,1,0:T(1,128)S(1)} %reshape.159), channel_id=1, replica_groups=mesh['snap'=32,'vert'=16] {'vert'}, dimensions={0} | all-to-all | bytes 1048576 | tf_op jit(solution)/shard_map/all_to_all | solution.py:29
  271.8 1.9 reduce.6
  273.7 3.5 %reshape.160 = f32[4096,1,32]{2,1,0:T(1,128)S(1)} reshape(f32[16,8192]{1,0:T(8,128)S(1)} %reduce.6) | data formatting | bytes 1048576
  277.2 0.7 copy.45
  277.9 0.3 copy.37
  278.2 0.2 copy.38
  278.4 2.1 fusion.22
  (10 shorter events, 0.2 us)
Async XLA Ops:
  6.5 1.0 copy-start
  6.5 16.4 %copy-start.5 = (s32[1,2]{1,0:T(1,128)S(1)}, s32[1,2]{1,0:T(1,128)}, u32[]{:S(2)}) copy-start(s32[1,2]{1,0:T(1,128)} %param.12) | copy-start | bytes 28
  6.5 16.5 %copy-start.4 = (s32[1,2,12]{2,1,0:T(2,128)S(1)}, s32[1,2,12]{2,1,0:T(2,128)}, u32[]{:S(2)}) copy-start(s32[1,2,12]{2,1,0:T(2,128)} %param.11) | copy-start | bytes 292
  6.5 88.0 %all-gather.2.cloned.1.call-start = ((), (), s32[]{:S(2)}) async-start(), calls=%async_computation.6 | async-start | bytes 13369344 | tf_op jit(solution)/shard_map/all_gather | solution.py:55
  12.8 31.8 %all-to-all-start = ((bf16[16,2,4096]{2,1,0:T(2,128)(2,1)}), bf16[16,2,4096]{2,1,0:T(2,128)(2,1)S(1)}, u32[]{:S(2)}, u32[]{:S(2)}) async-start(bf16[16,2,4096]{2,1,0:T(2,128)(2,1)} %reshape.151), calls=%async_computation | async-start | bytes 524288 | tf_op jit(solution)/shard_map/all_to_all | solution.py:20
  150.9 4.7 %copy-start.1 = (bf16[1,256,512]{2,1,0:T(8,128)(2,1)S(1)}, bf16[1,256,512]{2,1,0:T(8,128)(2,1)}, u32[]{:S(2)}) copy-start(bf16[1,256,512]{2,1,0:T(8,128)(2,1)} %param.9) | copy-start | bytes 786436
  155.1 16.7 %copy-start.3 = (f32[16,512]{1,0:T(8,128)S(1)}, f32[16,512]{1,0:T(8,128)}, u32[]{:S(2)}) copy-start(f32[16,512]{1,0:T(8,128)} %param.15) | copy-start | bytes 98308
  157.4 43.6 %copy-start.2 = (bf16[512,512]{1,0:T(8,128)(2,1)S(1)}, bf16[512,512]{1,0:T(8,128)(2,1)}, u32[]{:S(2)}) copy-start(bf16[512,512]{1,0:T(8,128)(2,1)} %param.16) | copy-start | bytes 1572868
  160.5 24.0 %all-to-all-start.2 = ((bf16[32,2,2048]{2,1,0:T(2,128)(2,1)}), bf16[32,2,2048]{2,1,0:T(2,128)(2,1)S(1)}, u32[]{:S(2)}, u32[]{:S(2)}) async-start(bf16[32,2,2048]{2,1,0:T(2,128)(2,1)} %reshape.155), calls=%async_computation.2 | async-start | bytes 524288 | tf_op jit(solution)/shard_map/all_to_all | solution.py:59
Sparse Core Ops, SparseCore 0:
  9.5 85.0 all-gather.1
where the time goes:
time: 291 us; the launch traced here: 288 us
  blocking collectives  94.9 us (33%)
  waiting for transfers between devices  60.2 us (21%)
  other arithmetic  50.3 us (17%)
  matrix products  25.4 us (9%)
  starting transfers between devices  21.5 us (7%)
  local copies, waits for them, and re-layouts  21.3 us (7%)
  between operations  14 us (5%)
    all_gather x1, waiting for transfers between devices, shards(): lax.all_gather(tile_values, 'vert', axis=1, tiled=True)  46.8 us
    unnamed x5, other arithmetic  45.4 us
    all_to_all x2, blocking collectives, aggregate(): lax.all_to_all(summed, 'vert', split_axis=1, concat_axis=2, tiled=True)  41.7 us
    all_gather x1, blocking collectives, shards(): lax.all_gather(table, 'vert', axis=1, tiled=True)  21.5 us
    dot_general x2, matrix products, aggregate(): jnp.einsum('srkij,srkjf->srif', tiles_all, picked, preferred_element_type...  16.9 us
    all_to_all x1, blocking collectives, aggregate(): lax.all_to_all(messages, 'vert', split_axis=2, concat_axis=1, tiled=True)  16.6 us
    unnamed x27, local copies, waits for them, and re-layouts  15.9 us
    all_to_all x1, blocking collectives, shards(): lax.all_to_all(mixed, 'snap', split_axis=0, concat_axis=1, tiled=True)  15.1 us
  transfers between devices with their start and end apart: 3, of which 2 were waited for; matrix products, arithmetic and copies ran while one was open for 3% of the time, Pallas kernels for 0%

commit v1 on v0

v1 whole, which is shorter than its diff:
```python
import jax
import jax.numpy as jnp
from jax import lax
from jax.experimental import pallas as pl
from jax.experimental.pallas import tpu as pltpu
from jax.sharding import PartitionSpec as P

TILE = 128
TAPS = 16


def layer_kernel(cols, counts, tiles, gathered, own, w_message, w_root, out, total):
    for r in range(2):
        total[r] = jnp.zeros(total.shape[1:], jnp.float32)

        @pl.loop(0, counts[r])
        def _(k):
            total[r] += jnp.dot(
                tiles[r, k], gathered[cols[r, k]], preferred_element_type=jnp.float32
            )

        rows = pl.ds(r * TILE, TILE)
        full = jnp.dot(
            total[r].astype(jnp.bfloat16), w_message[...], preferred_element_type=jnp.float32
        ) + jnp.dot(own[rows, :], w_root[...], preferred_element_type=jnp.float32)
        out[rows, :] = jnp.maximum(full, 0.0).astype(jnp.bfloat16)


def graph_layer(inputs, tiles, columns, counts, w_message, w_root):
    rows, width = inputs.shape
    gathered = lax.all_gather(inputs, "vert", axis=0, tiled=True)
    gathered = gathered.reshape(-1, TILE, width)
    smem = pl.BlockSpec(memory_space=pltpu.SMEM)
    vmem = pl.BlockSpec(memory_space=pltpu.VMEM)
    return pl.pallas_call(
        layer_kernel,
        out_shape=jax.ShapeDtypeStruct((rows, width), jnp.bfloat16),
        in_specs=[smem, smem, vmem, vmem, vmem, vmem, vmem],
        out_specs=vmem,
        scratch_shapes=[pltpu.VMEM((2, TILE, width), jnp.float32)],
        compiler_params=pltpu.CompilerParams(vmem_limit_bytes=24 << 20),
        name="layer",
    )(columns, counts, tiles, gathered, inputs, w_message, w_root)


def filter_kernel(hidden, taps, out):
    steps = hidden.shape[0]
    for t in range(steps):
        acc = taps[0:1, :] * hidden[t].astype(jnp.float32)
        for j in range(1, min(TAPS - 1, t) + 1):
            acc = acc + taps[j : j + 1, :] * hidden[t - j].astype(jnp.float32)
        out[t] = acc.astype(jnp.bfloat16)


def temporal(hidden, taps):
    rows, width = hidden.shape
    steps = lax.axis_size("snap")
    split = hidden.reshape(steps, rows // steps, width)
    by_vertex = lax.all_to_all(split, "snap", split_axis=0, concat_axis=0)
    vmem = pl.BlockSpec(memory_space=pltpu.VMEM)
    mixed = pl.pallas_call(
        filter_kernel,
        out_shape=jax.ShapeDtypeStruct(by_vertex.shape, jnp.bfloat16),
        in_specs=[vmem, vmem],
        out_specs=vmem,
        name="temporal",
    )(by_vertex, taps)
    returned = lax.all_to_all(mixed, "snap", split_axis=0, concat_axis=0)
    return returned.reshape(rows, width)


def shards(
    features,
    tile_values,
    tile_column,
    tile_count,
    message_one,
    root_one,
    time_taps,
    message_two,
    root_two,
):
    tiles, columns, counts = tile_values[0], tile_column[0], tile_count[0]
    hidden = graph_layer(features[0], tiles, columns, counts, message_one, root_one)
    mixed = temporal(hidden, time_taps)
    out = graph_layer(mixed, tiles, columns, counts, message_two, root_two)
    return out[None]


def solution(mesh):
    return jax.shard_map(
        shards,
        mesh=mesh,
        in_specs=(
            P("snap", "vert", None),
            P("snap", "vert", None, None, None),
            P("snap", "vert", None),
            P("snap", "vert"),
            P(),
            P(),
            P(),
            P(),
            P(),
        ),
        out_specs=P("snap", "vert", None),
        check_vma=False,
    )
```

time: 291 us -> 167 us (0.57)
  blocking collectives: 94.9 us -> 40.4 us
  other arithmetic: 50.3 us -> 0 us
  waiting for transfers between devices: 60.2 us -> 90.7 us
  matrix products: 25.4 us -> 0 us
  starting transfers between devices: 21.5 us -> 0.04 us
  local copies, waits for them, and re-layouts: 21.3 us -> 10.8 us
  Pallas kernels: 0 us -> 8.51 us
    unnamed x5 -> x0, other arithmetic: 45.4 us -> none
    all_gather x1 -> x2, waiting for transfers between devices: 46.8 us -> 90 us  [graph_layer(): gathered = lax.all_gather(inputs, 'vert', axis=0, tiled=True)]
    all_to_all x4 -> x2, blocking collectives: 73.4 us -> 40.4 us  [the longest x1 24.1 us: temporal(): by_vertex = lax.all_to_all(split, 'snap', split_axis=0, concat_axis=0)]
    dot_general x8 -> x0, matrix products: 25.4 us -> none  [the longest x2 16.9 us: aggregate(): jnp.einsum('srkij,srkjf->srif', tiles_all, picked, preferred_element_type...]
    all_gather x1 -> x0, blocking collectives: 21.5 us -> none  [shards(): lax.all_gather(table, 'vert', axis=1, tiled=True)]
    all_to_all x2 -> x0, starting transfers between devices: 21.5 us -> none  [the longest x1 11.3 us: shards(): lax.all_to_all(hidden, 'snap', split_axis=1, concat_axis=0, tiled=True)]
    all_to_all x2 -> x0, waiting for transfers between devices: 12.7 us -> none  [the longest x1 12.7 us: shards(): lax.all_to_all(hidden, 'snap', split_axis=1, concat_axis=0, tiled=True)]
    pallas_call x0 -> x3, Pallas kernels: none -> 8.51 us  [the longest x2 6.27 us: graph_layer(): pl.pallas_call(layer_kernel, out_shape=jax.ShapeDtypeStruct((rows, width)...]
  transfers between devices with their start and end apart: 3 -> 2, of which waited for: 2 -> 2; matrix products, arithmetic and copies ran while one was open for 3% -> 0% of each run, Pallas kernels for 0% -> 0%
where the time goes in v1:
time: 167 us; the launch traced here: 164 us
  waiting for transfers between devices  90.7 us (54%)
  blocking collectives  40.4 us (24%)
  between operations  13.5 us (8%)
  local copies, waits for them, and re-layouts  10.8 us (6%)
  Pallas kernels  8.51 us (5%)
    all_gather x2, waiting for transfers between devices, graph_layer(): gathered = lax.all_gather(inputs, 'vert', axis=0, tiled=True)  90 us
    all_to_all x1, blocking collectives, temporal(): by_vertex = lax.all_to_all(split, 'snap', split_axis=0, concat_axis=0)  24.1 us
    all_to_all x1, blocking collectives, temporal(): returned = lax.all_to_all(mixed, 'snap', split_axis=0, concat_axis=0)  16.3 us
    unnamed x28, local copies, waits for them, and re-layouts  10.8 us
    pallas_call x2, Pallas kernels, graph_layer(): pl.pallas_call(layer_kernel, out_shape=jax.ShapeDtypeStruct((rows, width)...  6.27 us
  transfers between devices with their start and end apart: 2, of which 2 were waited for; matrix products, arithmetic and copies ran while one was open for 0% of the time, Pallas kernels for 0%

profile of v1, /device:TPU:1, one launch (start us, length us, event | category | flops | bytes accessed | tf_op | source)
XLA Modules:
  0.0 163.9 jit_solution(10077603139550812666)
XLA Ops:
  6.5 0.0 all-gather.6.cloned.1.call-start
  6.5 0.7 all-gather.6.cloned.1.call-update
  7.3 0.0 all-gather.4.cloned.1.call-start
  7.3 52.4 %all-gather.6.cloned.1.call-done = bf16[1,4096,512]{2,1,0:T(8,128)(2,1)} async-done(((bf16[1,256,512]{2,1,0:T(8,128)(2,1)}), bf16[1,4096,512]{2,1,0:T(8,128)(2,1)}) %all-gather.6.cloned.1.call-update) | async-done | bytes 4194320 | tf_op jit(solution)/shard_map/all_gather | solution.py:31
  59.7 0.0 copy-start
  59.7 2.2 %copy-done = bf16[1,4096,512]{2,1,0:T(8,128)(2,1)S(1)} copy-done((bf16[1,4096,512]{2,1,0:T(8,128)(2,1)S(1)}, bf16[1,4096,512]{2,1,0:T(8,128)(2,1)}, u32[]{:S(2)}) %copy-start) | copy-done | bytes 4194328
  61.9 0.0 copy-start.2
  61.9 1.1 copy-done.2
  63.1 0.0 copy-start.5
  63.1 0.9 copy-done.5
  64.0 0.0 copy-start.6
  64.0 1.0 copy-done.6
  65.0 0.0 copy-start.7
  65.1 1.0 copy-done.7
  66.1 0.0 copy-start.10
  66.1 0.7 copy-done.10
  66.8 0.0 copy-start.12
  66.8 0.7 copy-done.12
  67.4 0.0 copy-start.3
  67.4 0.0 copy-start.8
  67.4 0.0 copy-start.9
  67.4 0.0 copy-start.11
  67.4 0.0 copy-start.13
  67.4 2.8 %layer.2 = bf16[256,512]{1,0:T(8,128)(2,1)S(1)} custom-call(s32[2,12]{1,0:T(2,128)S(1)} %bitcast.17, s32[2]{0:T(128)S(1)} %bitcast.19, bf16[2,12,128,128]{3,2,1,0:T(8,128)(2,1)S(1)} %bitcast.11, bf16[32,128,512]{2,1,0:T(8,128)(2,1)S(1)} %bitcast.9, bf16[256,512]{1,0:T(8,128)(2,1)S(1)} %bitcast.15, bf16[512,512]{1,0:T(8,128)(2,1)S(1)} %copy-done.6, ...), custom_call_target="tpu_custom_call" | custom-call | tf_op jit(solution)/shard_map/layer/pallas_call | solution.py:35
  70.2 24.1 %all_to_all.10.hidden = bf16[32,8,512]{2,1,0:T(8,128)(2,1)} all-to-all(bf16[32,8,512]{2,1,0:T(8,128)(2,1)S(1)} %bitcast.16), channel_id=1, replica_groups=mesh['snap'=32,'vert'=16] {'snap'}, dimensions={0} | all-to-all | bytes 524288 | tf_op jit(solution)/shard_map/all_to_all | solution.py:59
  94.3 2.2 %temporal.1 = bf16[32,8,512]{2,1,0:T(8,128)(2,1)} custom-call(bf16[32,8,512]{2,1,0:T(8,128)(2,1)} %all_to_all.10.hidden, f32[16,512]{1,0:T(8,128)} %taps.1), custom_call_target="tpu_custom_call" | custom-call | tf_op jit(solution)/shard_map/temporal/pallas_call | solution.py:61
  96.6 16.3 %all_to_all.11 = bf16[32,8,512]{2,1,0:T(8,128)(2,1)} all-to-all(bf16[32,8,512]{2,1,0:T(8,128)(2,1)} %temporal.1), channel_id=1, replica_groups=mesh['snap'=32,'vert'=16] {'snap'}, dimensions={0} | all-to-all | bytes 524288 | tf_op jit(solution)/shard_map/all_to_all | solution.py:68
  112.9 0.0 all-gather.4.cloned.1.call-update
  112.9 37.5 %all-gather.4.cloned.1.call-done = bf16[4096,512]{1,0:T(8,128)(2,1)} async-done(((bf16[256,512]{1,0:T(8,128)(2,1)}), bf16[4096,512]{1,0:T(8,128)(2,1)}) %all-gather.4.cloned.1.call-update) | async-done | bytes 4194320 | tf_op jit(solution)/shard_map/all_gather | solution.py:31
  150.4 0.0 copy-done.3
  150.4 0.0 copy-done.8
  150.4 0.0 copy-done.9
  150.5 0.0 copy-done.11
  150.5 0.0 copy-done.13
  150.5 0.0 copy-start.1
  150.5 2.2 %copy-done.1 = bf16[4096,512]{1,0:T(8,128)(2,1)S(1)} copy-done((bf16[4096,512]{1,0:T(8,128)(2,1)S(1)}, bf16[4096,512]{1,0:T(8,128)(2,1)}, u32[]{:S(2)}) %copy-start.1) | copy-done | bytes 4194328
  152.7 0.0 copy-start.4
  152.7 0.9 copy-done.4
  153.6 3.5 %layer.3 = bf16[256,512]{1,0:T(8,128)(2,1)} custom-call(s32[2,12]{1,0:T(2,128)S(1)} %bitcast.18, s32[2]{0:T(128)S(1)} %bitcast.20, bf16[2,12,128,128]{3,2,1,0:T(8,128)(2,1)S(1)} %bitcast.12, bf16[32,128,512]{2,1,0:T(8,128)(2,1)S(1)} %bitcast.10, bf16[256,512]{1,0:T(8,128)(2,1)S(1)} %bitcast.14, bf16[512,512]{1,0:T(8,128)(2,1)S(1)} %copy-done.8, ...), custom_call_target="tpu_custom_call" | custom-call | tf_op jit(solution)/shard_map/layer/pallas_call | solution.py:35
Async XLA Ops:
  6.5 53.2 %all-gather.6.cloned.1.call-start = ((), (), s32[]{:S(2)}) async-start(), calls=%async_computation.3 | async-start | bytes 4456448 | tf_op jit(solution)/shard_map/all_gather | solution.py:31
  7.3 143.2 %all-gather.4.cloned.1.call-start = ((), (), s32[]{:S(2)}) async-start(), calls=%async_computation.2 | async-start | bytes 4456448 | tf_op jit(solution)/shard_map/all_gather | solution.py:31
  59.7 2.2 %copy-start = (bf16[1,4096,512]{2,1,0:T(8,128)(2,1)S(1)}, bf16[1,4096,512]{2,1,0:T(8,128)(2,1)}, u32[]{:S(2)}) copy-start(bf16[1,4096,512]{2,1,0:T(8,128)(2,1)} %all-gather.6.cloned.1.call-done) | copy-start | bytes 12582916
  61.9 1.1 copy-start.2
  63.1 0.9 copy-start.5
  64.0 1.0 copy-start.6
  65.0 1.0 copy-start.7
  66.1 0.7 copy-start.10
  66.8 0.7 copy-start.12
  67.4 83.0 %copy-start.3 = (bf16[1,2,12,128,128]{4,3,2,1,0:T(8,128)(2,1)S(1)}, bf16[1,2,12,128,128]{4,3,2,1,0:T(8,128)(2,1)}, u32[]{:S(2)}) copy-start(bf16[1,2,12,128,128]{4,3,2,1,0:T(8,128)(2,1)} %param.10) | copy-start | bytes 2359300
  67.4 83.0 %copy-start.8 = (bf16[512,512]{1,0:T(8,128)(2,1)S(1)}, bf16[512,512]{1,0:T(8,128)(2,1)}, u32[]{:S(2)}) copy-start(bf16[512,512]{1,0:T(8,128)(2,1)} %w_message.3) | copy-start | bytes 1572868
  67.4 83.0 %copy-start.9 = (bf16[512,512]{1,0:T(8,128)(2,1)S(1)}, bf16[512,512]{1,0:T(8,128)(2,1)}, u32[]{:S(2)}) copy-start(bf16[512,512]{1,0:T(8,128)(2,1)} %w_root.3) | copy-start | bytes 1572868
  67.4 83.0 %copy-start.11 = (s32[1,2,12]{2,1,0:T(2,128)S(1)}, s32[1,2,12]{2,1,0:T(2,128)}, u32[]{:S(2)}) copy-start(s32[1,2,12]{2,1,0:T(2,128)} %param.11) | copy-start | bytes 292
  67.4 83.0 %copy-start.13 = (s32[1,2]{1,0:T(1,128)S(1)}, s32[1,2]{1,0:T(1,128)}, u32[]{:S(2)}) copy-start(s32[1,2]{1,0:T(1,128)} %param.12) | copy-start | bytes 28
  150.5 2.2 %copy-start.1 = (bf16[4096,512]{1,0:T(8,128)(2,1)S(1)}, bf16[4096,512]{1,0:T(8,128)(2,1)}, u32[]{:S(2)}) copy-start(bf16[4096,512]{1,0:T(8,128)(2,1)} %all-gather.4.cloned.1.call-done) | copy-start | bytes 12582916
  152.7 0.9 copy-start.4
Sparse Core Ops, SparseCore 0:
  9.4 50.2 all-gather.5
  113.0 37.3 all-gather.3
